TPU v7x, 256 devices: a whole 4x4x8 slice. The times are simulated.
256 devices in a mesh: blk: 64 (over x, z, y_hi), col: 4 (over y_lo, core).
Axes of the slice: x: 4, y: 4 (y_hi: 2, y_lo: 2; y = y_hi * 2 + y_lo), z: 8, core: 2. Of those that a mesh axis runs over, the one named last changes fastest.
Arguments:
- points: bfloat16 [32768, 128], P(('blk', 'col')), may hold values from -4.5 to 4.5
- targets: float32 [32768, 32], P(('blk', 'col')), may hold values from -6 to 6
- pivots: int32 [2, 256], replicated, may hold values from 0 to 32767, as said below
Outputs:
- factor: bfloat16 [32768, 512], P(('blk', 'col'))
- solution: float32 [32768, 32], P(('blk', 'col'))
- residual: float32 [32768, 32], P(('blk', 'col'))
Inputs may be any that keep to these rules, and one draw needn't show every extreme that they name: `pivots`: the 512 indices are distinct; 0 and 32767 are among them.
All inputs are finite; a program needn't handle non-finite values.
Results may differ from a plain program's by a relative error of at most 0.012.
Values may be sent and summed in bfloat16 or wider, within the bound.
No kernel may reach another device: no remote copies, remote signals or barrier semaphores. Data moves between devices by JAX's collectives and lax.ppermute only.
A program may use at most 64 MiB of HBM per device.

v0:
```python
import jax
import jax.numpy as jnp
from jax import lax
from jax.sharding import PartitionSpec as P

FEATURES = 128
ITERS = 3
noise_level = 0.5
jitter_level = 0.05
highest = lax.Precision.HIGHEST


def squared_norms(point_rows):
    wide_rows = point_rows.astype(jnp.float32)
    return jnp.sum(wide_rows * wide_rows, axis=1)


def kernel_block(left_rows, left_norms, right_rows, right_norms):
    inner = lax.dot_general(
        left_rows, right_rows, (((1,), (1,)), ((), ())), preferred_element_type=jnp.float32
    )
    distance = left_norms[:, None] + right_norms[None, :] - 2.0 * inner
    return jnp.exp(-2.0 * distance / FEATURES)


def lower_solve(lower_factor, right_rows):
    return jax.scipy.linalg.solve_triangular(lower_factor, right_rows.T, lower=True).T


def build_factor(point_rows, first_pick, second_pick):
    row_norms = squared_norms(point_rows)
    first_norms = squared_norms(first_pick)
    second_norms = squared_norms(second_pick)
    identity_piv = jnp.eye(first_pick.shape[0], dtype=jnp.float32)
    first_chol = jnp.linalg.cholesky(
        kernel_block(first_pick, first_norms, first_pick, first_norms) + jitter_level * identity_piv
    )
    first_coef = lower_solve(
        first_chol, kernel_block(point_rows, row_norms, first_pick, first_norms)
    )
    shared_coef = lower_solve(
        first_chol, kernel_block(second_pick, second_norms, first_pick, first_norms)
    )
    schur_block = (
        kernel_block(second_pick, second_norms, second_pick, second_norms)
        + jitter_level * identity_piv
        - jnp.dot(shared_coef, shared_coef.T, precision=highest)
    )
    second_chol = jnp.linalg.cholesky(schur_block)
    second_cross = kernel_block(point_rows, row_norms, second_pick, second_norms) - jnp.dot(
        first_coef, shared_coef.T, precision=highest
    )
    second_coef = lower_solve(second_chol, second_cross)
    return jnp.concatenate([first_coef, second_coef], axis=1)


def per_device(points, targets, pivots):
    row_count = points.shape[0]
    piv_count = pivots.shape[1]
    shard_index = lax.axis_index("blk") * lax.axis_size("col") + lax.axis_index("col")
    first_row = shard_index * row_count
    flat_pivots = pivots.reshape(-1)
    owned = (
        flat_pivots[:, None] == first_row + jnp.arange(row_count, dtype=jnp.int32)[None, :]
    ).astype(jnp.float32)
    local_pick = jnp.dot(owned, points.astype(jnp.float32), precision=highest)
    picked = lax.psum(local_pick, ("blk", "col")).astype(jnp.bfloat16)
    wide_factor = build_factor(points, picked[:piv_count], picked[piv_count:])
    factor = wide_factor.astype(jnp.bfloat16)
    local_gram = lax.dot_general(
        wide_factor, wide_factor, (((0,), (0,)), ((), ())), precision=highest
    )
    gram = lax.psum(local_gram, ("blk", "col"))
    gram = gram + noise_level * jnp.eye(2 * piv_count, dtype=jnp.float32)
    gram_chol = jnp.linalg.cholesky(gram)

    def precondition(residual_now):
        local_proj = lax.dot_general(
            wide_factor, residual_now, (((0,), (0,)), ((), ())), precision=highest
        )
        projection = lax.psum(local_proj, ("blk", "col"))
        coefficients = jax.scipy.linalg.cho_solve((gram_chol, True), projection)
        scaled = (
            residual_now - jnp.dot(wide_factor, coefficients, precision=highest)
        ) / noise_level
        return (scaled, lax.psum(jnp.sum(residual_now * scaled, axis=0), ("blk", "col")))

    own_block = lax.all_gather(points, "col", axis=0, tiled=True)
    own_norms = squared_norms(own_block)

    def tile_add(total, key_rows, key_norms, direction_rows):
        weights = kernel_block(own_block, own_norms, key_rows, key_norms)
        return total + jnp.dot(weights, direction_rows, precision=highest)

    solution = jnp.zeros_like(targets)
    residual = targets
    direction_now, inner_now = precondition(residual)
    for step_index in range(ITERS):
        empty = jnp.zeros((own_block.shape[0], direction_now.shape[1]), jnp.float32)
        add_key_rows = lax.all_gather(points.astype(jnp.float32), "blk", axis=0, tiled=True).astype(
            jnp.bfloat16
        )
        fold_direction_rows = lax.all_gather(direction_now, "blk", axis=0, tiled=True)
        piece_rows = add_key_rows.shape[0]
        splits = piece_rows // row_count

        def scan_step(carry, operands):
            return (tile_add(carry, operands[0], operands[1], operands[2]), None)

        stacked = (
            add_key_rows.reshape(splits, row_count, add_key_rows.shape[1]),
            squared_norms(add_key_rows).reshape(splits, row_count),
            fold_direction_rows.reshape(splits, row_count, fold_direction_rows.shape[1]),
        )
        result, unused = lax.scan(scan_step, empty, stacked)
        image = (
            lax.psum_scatter(result, "col", scatter_dimension=0, tiled=True)
            + noise_level * direction_now
        )
        curvature = lax.psum(jnp.sum(direction_now * image, axis=0), ("blk", "col"))
        step_size = inner_now / curvature
        solution = solution + step_size * direction_now
        residual = residual - step_size * image
        if step_index + 1 < ITERS:
            scaled, inner_next = precondition(residual)
            direction_now = scaled + inner_next / inner_now * direction_now
            inner_now = inner_next
    return (factor, solution, residual)


def solution(mesh):
    return jax.shard_map(
        per_device,
        mesh=mesh,
        in_specs=(P(("blk", "col"), None), P(("blk", "col"), None), P()),
        out_specs=(P(("blk", "col"), None), P(("blk", "col"), None), P(("blk", "col"), None)),
        check_vma=False,
    )
```

profile of v0, /device:TPU:1, one launch (start us, length us, event | category | flops | bytes accessed | tf_op | source)
XLA Modules:
  0.0 2410.5 jit_solution(17141482593332180947)
XLA Ops:
  8.9 82.6 %all-reduce.14 = bf16[512,128]{1,0:T(8,128)(2,1)S(1)} all-reduce(f32[512,128]{1,0:T(8,128)S(1)} %fusion.57), channel_id=1, replica_groups=mesh['blk'=64,'col'=4] {'blk','col'}, use_global_device_ids=true, to_apply=%region_0.0 | all-reduce | flops 65536 | bytes 393216 | tf_op jit(solution)/shard_map/psum | solution.py:67
  133.6 19.7 custom-call.55
  178.1 11.7 cholesky.391
  196.9 19.7 custom-call.57
  221.1 251.4 %all-reduce.13.cloned.1.call-done = (f32[512,512]{1,0:T(8,128)}, f32[512,32]{0,1:T(8,128)}) async-done(((f32[512,512]{1,0:T(8,128)}, f32[512,32]{0,1:T(8,128)}), (f32[512,512]{1,0:T(8,128)}, f32[512,32]{0,1:T(8,128)})) %all-reduce.13.cloned.1.call-update) | async-done | bytes 1114128 | tf_op jit(solution)/shard_map/psum | solution.py:73
  543.4 11.7 cholesky.305
  569.1 40.1 %custom-call.59 = f32[4,128,128]{1,2,0:T(8,128)S(1)} custom-call(f32[4,128,128]{2,1,0:T(8,128)} %get-tuple-element.393), custom_call_target="InvertDiagBlocksLowerTriangular" | custom-call | tf_op jit(solution)/shard_map/jit(_cho_solve)/triangular_solve | solution.py:82
  621.0 92.2 %all-gather.7.cloned.1.call-done = f32[8192,32]{0,1:T(8,128)} async-done(((f32[128,32]{0,1:T(8,128)}), f32[8192,32]{0,1:T(8,128)}) %all-gather.7.cloned.1.call-update) | async-done | bytes 1048592 | tf_op jit(solution)/shard_map/all_gather | solution.py:103
  716.7 116.0 %all-gather.5.cloned.1.call-done = bf16[8192,128]{1,0:T(8,128)(2,1)} async-done(((bf16[128,128]{1,0:T(8,128)(2,1)}), bf16[8192,128]{1,0:T(8,128)(2,1)}) %all-gather.5.cloned.1.call-update) | async-done | bytes 2097168 | tf_op jit(solution)/shard_map/all_gather | solution.py:100
  835.5 144.7 %while.50 = (s32[]{:T(128)}, f32[512,32]{0,1:T(8,128)S(1)}, f32[512]{0:T(512)S(1)}, f32[64,128]{1,0:T(8,128)S(1)}, bf16[64,128,128]{2,1,0:T(8,128)(2,1)}, /*inde...) while((s32[]{:T(128)}, f32[512,32]{0,1:T(8,128)S(1)}, ...), condition=%wide.region_23.28_spmd.clone, body=%wide.region_22.27_spmd.clone.sunk | while | flops 42237952 | bytes 889451 | solution.py:115
  980.9 20.1 reduce-scatter.4.cloned.1.call-done
  1001.8 77.0 %all-reduce.2 = (f32[32]{0:T(128)S(1)}, f32[32]{0:T(128)S(1)}) all-reduce(f32[32]{0:T(128)S(1)} %get-tuple-element.431, f32[32]{0:T(128)S(1)} %get-tuple-element.430), channel_id=1, replica_groups=mesh['blk'=64,'col'=4] {'blk','col'}, use_global_device_ids=true, to_apply=%region_19.24 | all-reduce | flops 64 | bytes 512 | tf_op jit(solution)/shard_map/psum | solution.py:86
  1079.9 234.4 %all-reduce.9.cloned.1.call-done = f32[512,32]{0,1:T(8,128)} async-done(((f32[512,32]{0,1:T(8,128)}), f32[512,32]{0,1:T(8,128)}) %all-reduce.9.cloned.1.call-update) | async-done | bytes 65552 | tf_op jit(solution)/shard_map/psum | solution.py:81
  1320.8 74.4 %psum.83 = f32[32]{0:T(128)S(1)} all-reduce(f32[32]{0:T(128)S(1)} %get-tuple-element.537), channel_id=1, replica_groups=mesh['blk'=64,'col'=4] {'blk','col'}, use_global_device_ids=true, to_apply=%region_29.34 | all-reduce | flops 32 | bytes 256 | tf_op jit(solution)/shard_map/psum | solution.py:86
  1396.0 95.6 %all-gather.9.cloned.1.call-done = f32[8192,32]{0,1:T(8,128)} async-done(((f32[128,32]{0,1:T(8,128)}), f32[8192,32]{0,1:T(8,128)}) %all-gather.9.cloned.1.call-update) | async-done | bytes 1048592 | tf_op jit(solution)/shard_map/all_gather | solution.py:103
  1495.1 144.7 %while.51 = (s32[]{:T(128)}, f32[512,32]{0,1:T(8,128)S(1)}, f32[512]{0:T(512)S(1)}, f32[64,128]{1,0:T(8,128)S(1)}, bf16[64,128,128]{2,1,0:T(8,128)(2,1)}, /*inde...) while((s32[]{:T(128)}, f32[512,32]{0,1:T(8,128)S(1)}, ...), condition=%wide.region_31.36_spmd.clone, body=%wide.region_30.35_spmd.clone.sunk | while | flops 42237952 | bytes 889451 | solution.py:115
  1640.5 21.1 reduce-scatter.6.cloned.1.call-done
  1662.4 77.3 %psum.84 = f32[32]{0:T(128)S(1)} all-reduce(f32[32]{0:T(128)S(1)} %multiply_reduce_fusion.7), channel_id=1, replica_groups=mesh['blk'=64,'col'=4] {'blk','col'}, use_global_device_ids=true, to_apply=%region_34.39 | all-reduce | flops 32 | bytes 256 | tf_op jit(solution)/shard_map/psum | solution.py:120
  1741.6 234.4 %all-reduce.11.cloned.1.call-done = f32[512,32]{0,1:T(8,128)} async-done(((f32[512,32]{0,1:T(8,128)}), f32[512,32]{0,1:T(8,128)}) %all-reduce.11.cloned.1.call-update) | async-done | bytes 65552 | tf_op jit(solution)/shard_map/psum | solution.py:81
  1982.4 74.4 %psum.86 = f32[32]{0:T(128)S(1)} all-reduce(f32[32]{0:T(128)S(1)} %get-tuple-element.539), channel_id=1, replica_groups=mesh['blk'=64,'col'=4] {'blk','col'}, use_global_device_ids=true, to_apply=%region_37.42 | all-reduce | flops 32 | bytes 256 | tf_op jit(solution)/shard_map/psum | solution.py:86
  2057.6 95.6 %all-gather.11.cloned.1.call-done = f32[8192,32]{0,1:T(8,128)} async-done(((f32[128,32]{0,1:T(8,128)}), f32[8192,32]{0,1:T(8,128)}) %all-gather.11.cloned.1.call-update) | async-done | bytes 1048592 | tf_op jit(solution)/shard_map/all_gather | solution.py:103
  2156.8 144.7 %while.52 = (s32[]{:T(128)}, f32[512,32]{0,1:T(8,128)S(1)}, f32[512]{0:T(512)S(1)}, f32[64,128]{1,0:T(8,128)S(1)}, bf16[64,128,128]{2,1,0:T(8,128)(2,1)}, /*inde...) while((s32[]{:T(128)}, f32[512,32]{0,1:T(8,128)S(1)}, ...), condition=%wide.region_39.44_spmd.clone, body=%wide.region_38.43_spmd.clone.sunk | while | flops 42237952 | bytes 889451 | solution.py:115
  2302.1 21.1 reduce-scatter.8.cloned.1.call-done
  2324.8 77.0 %psum.87 = f32[32]{0:T(128)S(1)} all-reduce(f32[32]{0:T(128)S(1)} %multiply_reduce_fusion.5), channel_id=1, replica_groups=mesh['blk'=64,'col'=4] {'blk','col'}, use_global_device_ids=true, to_apply=%region_42.47 | all-reduce | flops 32 | bytes 256 | tf_op jit(solution)/shard_map/psum | solution.py:120
  (807 shorter events, 652.9 us)
Async XLA Ops:
  7.2 119.0 %copy-start.5 = (bf16[128,128]{1,0:T(8,128)(2,1)S(1)}, bf16[128,128]{1,0:T(8,128)(2,1)}, u32[]{:S(2)}) copy-start(bf16[128,128]{1,0:T(8,128)(2,1)} %param.16) | copy-start | bytes 98308
  7.2 465.3 %all-reduce.13.cloned.1.call-start = ((), (), s32[]{:S(2)}) async-start(), calls=%async_computation.12 | async-start | bytes 2228224 | tf_op jit(solution)/shard_map/psum | solution.py:73
  154.5 65.5 %copy-start.8 = (f32[128,32]{0,1:T(8,128)S(1)}, f32[128,32]{0,1:T(8,128)}, u32[]{:S(2)}) copy-start(f32[128,32]{0,1:T(8,128)} %param.17) | copy-start | bytes 49156
  221.1 492.1 %all-gather.7.cloned.1.call-start = ((), (), s32[]{:S(2)}) async-start(), calls=%async_computation.4 | async-start | bytes 1064960 | tf_op jit(solution)/shard_map/all_gather | solution.py:103
  472.5 1.8 copy-start
  474.5 134.7 %copy-start.9 = (f32[512,32]{0,1:T(8,128)S(1)}, f32[512,32]{0,1:T(8,128)}, u32[]{:S(2)}) copy-start(f32[512,32]{0,1:T(8,128)} %get-tuple-element.501) | copy-start | bytes 196612
  496.5 117.6 %copy-start.6 = (bf16[128,128]{1,0:T(8,128)(2,1)S(1)}, bf16[128,128]{1,0:T(8,128)(2,1)}, u32[]{:S(2)}) copy-start(bf16[128,128]{1,0:T(8,128)(2,1)} %param.16) | copy-start | bytes 98308
  613.3 219.4 %all-gather.5.cloned.1.call-start = ((), (), s32[]{:S(2)}) async-start(), calls=%async_computation.3 | async-start | bytes 2129920 | tf_op jit(solution)/shard_map/all_gather | solution.py:100
  614.1 386.8 %reduce-scatter.4.cloned.1.call-start = ((), (), s32[]{:S(2)}) async-start(), calls=%async_computation.5 | async-start | bytes 81920 | tf_op jit(solution)/shard_map/reduce_scatter | solution.py:117
  980.2 0.6 copy-start.1
  980.8 333.5 %all-reduce.9.cloned.1.call-start = ((), (), s32[]{:S(2)}) async-start(), calls=%async_computation.6 | async-start | bytes 131072 | tf_op jit(solution)/shard_map/psum | solution.py:81
  1079.9 411.7 %all-gather.9.cloned.1.call-start = ((), (), s32[]{:S(2)}) async-start(), calls=%async_computation.7 | async-start | bytes 1064960 | tf_op jit(solution)/shard_map/all_gather | solution.py:103
  1395.9 265.7 %reduce-scatter.6.cloned.1.call-start = ((), (), s32[]{:S(2)}) async-start(), calls=%async_computation.8 | async-start | bytes 81920 | tf_op jit(solution)/shard_map/reduce_scatter | solution.py:117
  1396.0 265.6 %copy-start.4 = (f32[128,32]{0,1:T(8,128)S(1)}, f32[128,32]{0,1:T(8,128)}, u32[]{:S(2)}) copy-start(f32[128,32]{0,1:T(8,128)} %multiply_add_fusion.4) | copy-start | bytes 49156
  1639.8 0.6 copy-start.2
  1640.5 335.5 %all-reduce.11.cloned.1.call-start = ((), (), s32[]{:S(2)}) async-start(), calls=%async_computation.9 | async-start | bytes 131072 | tf_op jit(solution)/shard_map/psum | solution.py:81
  1741.5 411.7 %all-gather.11.cloned.1.call-start = ((), (), s32[]{:S(2)}) async-start(), calls=%async_computation.10 | async-start | bytes 1064960 | tf_op jit(solution)/shard_map/all_gather | solution.py:103
  2057.5 265.7 %reduce-scatter.8.cloned.1.call-start = ((), (), s32[]{:S(2)}) async-start(), calls=%async_computation.11 | async-start | bytes 81920 | tf_op jit(solution)/shard_map/reduce_scatter | solution.py:117
  2057.6 265.6 %copy-start.7 = (f32[128,32]{0,1:T(8,128)S(1)}, f32[128,32]{0,1:T(8,128)}, u32[]{:S(2)}) copy-start(f32[128,32]{0,1:T(8,128)} %multiply_add_fusion.2) | copy-start | bytes 49156
  2301.4 0.6 copy-start.3
Sparse Core Ops, SparseCore 0:
  221.2 251.2 all-reduce.12
  613.5 99.6 all-gather.6
  717.3 115.3 all-gather.4
  981.0 19.9 reduce-scatter.3
  1080.0 234.2 all-reduce.8
  1396.0 95.4 all-gather.8
  1640.6 20.9 reduce-scatter.5
  1741.6 234.2 all-reduce.10
  2057.6 95.4 all-gather.10
  2302.2 20.9 reduce-scatter.7
where the time goes:
time: 2440 us; the launch traced here: 2410 us
  waiting for transfers between devices  1180 us (48%)
  blocking collectives  469 us (19%)
  matrix products  455 us (19%)
  other arithmetic  239 us (10%)
  local copies, waits for them, and re-layouts  35.5 us (1%)
    psum x2, waiting for transfers between devices, precondition(): projection = lax.psum(local_proj, ('blk', 'col'))  469 us
    all_gather x3, waiting for transfers between devices, per_device(): lax.all_gather(direction_now, 'blk', axis=0, tiled=True)  283 us
    psum x1, waiting for transfers between devices, per_device(): gram = lax.psum(local_gram, ('blk', 'col'))  251 us
    dot_general x192, matrix products, tile_add(): return total + jnp.dot(weights, direction_rows, precision=highest)  238 us
    psum x3, blocking collectives, precondition(): lax.psum(jnp.sum(residual_now * scaled, axis=0), ('blk', 'col'))  226 us
    dot_general x197, matrix products, kernel_block(): lax.dot_general(left_rows, right_rows, (((1,), (1,)), ((), ())), preferre...  187 us
    psum x2, blocking collectives, per_device(): curvature = lax.psum(jnp.sum(direction_now * image, axis=0), ('blk', 'col'))  154 us
    all_gather x1, waiting for transfers between devices, per_device(): lax.all_gather(points.astype(jnp.float32), 'blk', axis=0, tiled=True)  116 us
  transfers between devices with their start and end apart: 10, of which 10 were waited for; matrix products, arithmetic and copies ran while one was open for 0% of the time, Pallas kernels for 0%

commit v1 on v0

--- a/solution.py
+++ b/solution.py
@@ -97,9 +97,12 @@
     direction_now, inner_now = precondition(residual)
     for step_index in range(ITERS):
         empty = jnp.zeros((own_block.shape[0], direction_now.shape[1]), jnp.float32)
-        add_key_rows = lax.all_gather(points.astype(jnp.float32), "blk", axis=0, tiled=True).astype(
-            jnp.bfloat16
-        )
+        add_key_rows = jnp.concatenate(
+            lax.all_to_all(
+                jnp.stack([points.astype(jnp.float32)] * lax.axis_size("blk")), "blk", 0, 0
+            ),
+            axis=0,
+        ).astype(jnp.bfloat16)
         fold_direction_rows = lax.all_gather(direction_now, "blk", axis=0, tiled=True)
         piece_rows = add_key_rows.shape[0]
         splits = piece_rows // row_count

time: 2440 us -> 2340 us (0.959)
  waiting for transfers between devices: 1180 us -> 1070 us
    all_gather x1 -> x0, waiting for transfers between devices: 116 us -> none  [per_device(): lax.all_gather(points.astype(jnp.float32), 'blk', axis=0, tiled=True)]
  transfers between devices with their start and end apart: 10 -> 10, of which waited for: 10 -> 9; matrix products, arithmetic and copies ran while one was open for 0% -> 6% of each run, Pallas kernels for 0% -> 0%
where the time goes in v1:
time: 2340 us; the launch traced here: 2310 us
  waiting for transfers between devices  1070 us (46%)
  blocking collectives  469 us (20%)
  matrix products  455 us (19%)
  other arithmetic  240 us (10%)
  local copies, waits for them, and re-layouts  37.3 us (2%)
    psum x2, waiting for transfers between devices, precondition(): projection = lax.psum(local_proj, ('blk', 'col'))  469 us
    all_gather x3, waiting for transfers between devices, per_device(): lax.all_gather(direction_now, 'blk', axis=0, tiled=True)  284 us
    psum x1, waiting for transfers between devices, per_device(): gram = lax.psum(local_gram, ('blk', 'col'))  254 us
    dot_general x192, matrix products, tile_add(): return total + jnp.dot(weights, direction_rows, precision=highest)  238 us
    psum x3, blocking collectives, precondition(): lax.psum(jnp.sum(residual_now * scaled, axis=0), ('blk', 'col'))  226 us
    dot_general x197, matrix products, kernel_block(): lax.dot_general(left_rows, right_rows, (((1,), (1,)), ((), ())), preferre...  187 us
    psum x2, blocking collectives, per_device(): curvature = lax.psum(jnp.sum(direction_now * image, axis=0), ('blk', 'col'))  154 us
    psum x1, blocking collectives, per_device(): picked = lax.psum(local_pick, ('blk', 'col')).astype(jnp.bfloat16)  82.6 us
  transfers between devices with their start and end apart: 10, of which 9 were waited for; matrix products, arithmetic and copies ran while one was open for 6% of the time, Pallas kernels for 0%

profile of v1, /device:TPU:1, one launch (start us, length us, event | category | flops | bytes accessed | tf_op | source)
XLA Modules:
  0.0 2307.6 jit_solution(2242038414064146537)
XLA Ops:
  9.8 82.6 %all-reduce.14 = bf16[512,128]{1,0:T(8,128)(2,1)S(1)} all-reduce(f32[512,128]{1,0:T(8,128)S(1)} %fusion.57), channel_id=1, replica_groups=mesh['blk'=64,'col'=4] {'blk','col'}, use_global_device_ids=true, to_apply=%region_0.0 | all-reduce | flops 65536 | bytes 393216 | tf_op jit(solution)/shard_map/psum | solution.py:67
  92.9 11.7 cholesky.354
  134.4 19.7 custom-call.55
  179.5 12.1 cholesky.391
  198.2 19.7 custom-call.57
  230.4 254.5 %all-reduce.13.cloned.1.call-done = (f32[512,512]{1,0:T(8,128)}, f32[512,32]{0,1:T(8,128)}) async-done(((f32[512,512]{1,0:T(8,128)}, f32[512,32]{0,1:T(8,128)}), (f32[512,512]{1,0:T(8,128)}, f32[512,32]{0,1:T(8,128)})) %all-reduce.13.cloned.1.call-update) | async-done | bytes 1114128 | tf_op jit(solution)/shard_map/psum | solution.py:73
  553.8 11.7 cholesky.305
  581.5 40.1 %custom-call.59 = f32[4,128,128]{1,2,0:T(8,128)S(1)} custom-call(f32[4,128,128]{2,1,0:T(8,128)} %get-tuple-element.393), custom_call_target="InvertDiagBlocksLowerTriangular" | custom-call | tf_op jit(solution)/shard_map/jit(_cho_solve)/triangular_solve | solution.py:82
  632.6 92.9 %all-gather.4.cloned.1.call-done = f32[8192,32]{0,1:T(8,128)} async-done(((f32[128,32]{0,1:T(8,128)}), f32[8192,32]{0,1:T(8,128)}) %all-gather.4.cloned.1.call-update) | async-done | bytes 1048592 | tf_op jit(solution)/shard_map/all_gather | solution.py:106
  731.9 144.7 %while.50 = (s32[]{:T(128)}, f32[512,32]{0,1:T(8,128)S(1)}, f32[512]{0:T(512)S(1)}, f32[64,128]{1,0:T(8,128)S(1)}, bf16[64,128,128]{2,1,0:T(8,128)(2,1)}, /*inde...) while((s32[]{:T(128)}, f32[512,32]{0,1:T(8,128)S(1)}, ...), condition=%wide.region_23.28_spmd.clone, body=%wide.region_22.27_spmd.clone.sunk | while | flops 42237952 | bytes 888443 | solution.py:118
  877.3 21.1 reduce-scatter.4.cloned.1.call-done
  899.2 77.0 %all-reduce.2 = (f32[32]{0:T(128)S(1)}, f32[32]{0:T(128)S(1)}) all-reduce(f32[32]{0:T(128)S(1)} %get-tuple-element.431, f32[32]{0:T(128)S(1)} %get-tuple-element.430), channel_id=1, replica_groups=mesh['blk'=64,'col'=4] {'blk','col'}, use_global_device_ids=true, to_apply=%region_19.24 | all-reduce | flops 64 | bytes 512 | tf_op jit(solution)/shard_map/psum | solution.py:86
  977.4 234.3 %all-reduce.9.cloned.1.call-done = f32[512,32]{0,1:T(8,128)} async-done(((f32[512,32]{0,1:T(8,128)}), f32[512,32]{0,1:T(8,128)}) %all-reduce.9.cloned.1.call-update) | async-done | bytes 65552 | tf_op jit(solution)/shard_map/psum | solution.py:81
  1218.1 74.4 %psum.83 = f32[32]{0:T(128)S(1)} all-reduce(f32[32]{0:T(128)S(1)} %get-tuple-element.537), channel_id=1, replica_groups=mesh['blk'=64,'col'=4] {'blk','col'}, use_global_device_ids=true, to_apply=%region_29.34 | all-reduce | flops 32 | bytes 256 | tf_op jit(solution)/shard_map/psum | solution.py:86
  1293.3 95.6 %all-gather.6.cloned.1.call-done = f32[8192,32]{0,1:T(8,128)} async-done(((f32[128,32]{0,1:T(8,128)}), f32[8192,32]{0,1:T(8,128)}) %all-gather.6.cloned.1.call-update) | async-done | bytes 1048592 | tf_op jit(solution)/shard_map/all_gather | solution.py:106
  1392.5 144.7 %while.51 = (s32[]{:T(128)}, f32[512,32]{0,1:T(8,128)S(1)}, f32[512]{0:T(512)S(1)}, f32[64,128]{1,0:T(8,128)S(1)}, bf16[64,128,128]{2,1,0:T(8,128)(2,1)}, /*inde...) while((s32[]{:T(128)}, f32[512,32]{0,1:T(8,128)S(1)}, ...), condition=%wide.region_31.36_spmd.clone, body=%wide.region_30.35_spmd.clone.sunk | while | flops 42237952 | bytes 888443 | solution.py:118
  1537.9 21.1 reduce-scatter.6.cloned.1.call-done
  1559.8 77.3 %psum.84 = f32[32]{0:T(128)S(1)} all-reduce(f32[32]{0:T(128)S(1)} %multiply_reduce_fusion.7), channel_id=1, replica_groups=mesh['blk'=64,'col'=4] {'blk','col'}, use_global_device_ids=true, to_apply=%region_34.39 | all-reduce | flops 32 | bytes 256 | tf_op jit(solution)/shard_map/psum | solution.py:123
  1638.9 234.4 %all-reduce.11.cloned.1.call-done = f32[512,32]{0,1:T(8,128)} async-done(((f32[512,32]{0,1:T(8,128)}), f32[512,32]{0,1:T(8,128)}) %all-reduce.11.cloned.1.call-update) | async-done | bytes 65552 | tf_op jit(solution)/shard_map/psum | solution.py:81
  1879.8 74.4 %psum.86 = f32[32]{0:T(128)S(1)} all-reduce(f32[32]{0:T(128)S(1)} %get-tuple-element.539), channel_id=1, replica_groups=mesh['blk'=64,'col'=4] {'blk','col'}, use_global_device_ids=true, to_apply=%region_37.42 | all-reduce | flops 32 | bytes 256 | tf_op jit(solution)/shard_map/psum | solution.py:86
  1955.0 95.6 %all-gather.8.cloned.1.call-done = f32[8192,32]{0,1:T(8,128)} async-done(((f32[128,32]{0,1:T(8,128)}), f32[8192,32]{0,1:T(8,128)}) %all-gather.8.cloned.1.call-update) | async-done | bytes 1048592 | tf_op jit(solution)/shard_map/all_gather | solution.py:106
  2054.1 144.7 %while.52 = (s32[]{:T(128)}, f32[512,32]{0,1:T(8,128)S(1)}, f32[512]{0:T(512)S(1)}, f32[64,128]{1,0:T(8,128)S(1)}, bf16[64,128,128]{2,1,0:T(8,128)(2,1)}, /*inde...) while((s32[]{:T(128)}, f32[512,32]{0,1:T(8,128)S(1)}, ...), condition=%wide.region_39.44_spmd.clone, body=%wide.region_38.43_spmd.clone.sunk | while | flops 42237952 | bytes 888443 | solution.py:118
  2199.5 21.1 reduce-scatter.8.cloned.1.call-done
  2222.2 77.0 %psum.87 = f32[32]{0:T(128)S(1)} all-reduce(f32[32]{0:T(128)S(1)} %multiply_reduce_fusion.5), channel_id=1, replica_groups=mesh['blk'=64,'col'=4] {'blk','col'}, use_global_device_ids=true, to_apply=%region_42.47 | all-reduce | flops 32 | bytes 256 | tf_op jit(solution)/shard_map/psum | solution.py:123
  (805 shorter events, 649.3 us)
Async XLA Ops:
  7.2 120.1 %copy-start.5 = (bf16[128,128]{1,0:T(8,128)(2,1)S(1)}, bf16[128,128]{1,0:T(8,128)(2,1)}, u32[]{:S(2)}) copy-start(bf16[128,128]{1,0:T(8,128)(2,1)} %param.16) | copy-start | bytes 98308
  7.2 477.7 %all-reduce.13.cloned.1.call-start = ((), (), s32[]{:S(2)}) async-start(), calls=%async_computation.12 | async-start | bytes 2228224 | tf_op jit(solution)/shard_map/psum | solution.py:73
  155.4 65.4 %copy-start.7 = (f32[128,32]{0,1:T(8,128)S(1)}, f32[128,32]{0,1:T(8,128)}, u32[]{:S(2)}) copy-start(f32[128,32]{0,1:T(8,128)} %param.17) | copy-start | bytes 49156
  223.6 505.5 %all-to-all-start = ((bf16[64,128,128]{2,1,0:T(8,128)(2,1)}), bf16[64,128,128]{2,1,0:T(8,128)(2,1)}, u32[]{:S(2)}, u32[]{:S(2)}) async-start(bf16[64,128,128]{2,1,0:T(8,128)(2,1)} %stack.2), calls=%async_computation | async-start | bytes 4194304 | tf_op jit(solution)/shard_map/all_to_all | solution.py:101
  230.4 495.1 %all-gather.4.cloned.1.call-start = ((), (), s32[]{:S(2)}) async-start(), calls=%async_computation.4 | async-start | bytes 1064960 | tf_op jit(solution)/shard_map/all_gather | solution.py:106
  484.9 1.8 copy-start
  486.9 134.7 %copy-start.8 = (f32[512,32]{0,1:T(8,128)S(1)}, f32[512,32]{0,1:T(8,128)}, u32[]{:S(2)}) copy-start(f32[512,32]{0,1:T(8,128)} %get-tuple-element.501) | copy-start | bytes 196612
  625.7 272.6 %reduce-scatter.4.cloned.1.call-start = ((), (), s32[]{:S(2)}) async-start(), calls=%async_computation.5 | async-start | bytes 81920 | tf_op jit(solution)/shard_map/reduce_scatter | solution.py:120
  876.6 0.6 copy-start.1
  877.2 334.5 %all-reduce.9.cloned.1.call-start = ((), (), s32[]{:S(2)}) async-start(), calls=%async_computation.6 | async-start | bytes 131072 | tf_op jit(solution)/shard_map/psum | solution.py:81
  977.3 411.6 %all-gather.6.cloned.1.call-start = ((), (), s32[]{:S(2)}) async-start(), calls=%async_computation.7 | async-start | bytes 1064960 | tf_op jit(solution)/shard_map/all_gather | solution.py:106
  1293.3 265.7 %reduce-scatter.6.cloned.1.call-start = ((), (), s32[]{:S(2)}) async-start(), calls=%async_computation.8 | async-start | bytes 81920 | tf_op jit(solution)/shard_map/reduce_scatter | solution.py:120
  1293.3 265.6 %copy-start.4 = (f32[128,32]{0,1:T(8,128)S(1)}, f32[128,32]{0,1:T(8,128)}, u32[]{:S(2)}) copy-start(f32[128,32]{0,1:T(8,128)} %multiply_add_fusion.4) | copy-start | bytes 49156
  1537.2 0.6 copy-start.2
  1537.8 335.5 %all-reduce.11.cloned.1.call-start = ((), (), s32[]{:S(2)}) async-start(), calls=%async_computation.9 | async-start | bytes 131072 | tf_op jit(solution)/shard_map/psum | solution.py:81
  1638.9 411.6 %all-gather.8.cloned.1.call-start = ((), (), s32[]{:S(2)}) async-start(), calls=%async_computation.10 | async-start | bytes 1064960 | tf_op jit(solution)/shard_map/all_gather | solution.py:106
  1954.9 265.7 %reduce-scatter.8.cloned.1.call-start = ((), (), s32[]{:S(2)}) async-start(), calls=%async_computation.11 | async-start | bytes 81920 | tf_op jit(solution)/shard_map/reduce_scatter | solution.py:120
  1955.0 265.6 %copy-start.6 = (f32[128,32]{0,1:T(8,128)S(1)}, f32[128,32]{0,1:T(8,128)}, u32[]{:S(2)}) copy-start(f32[128,32]{0,1:T(8,128)} %multiply_add_fusion.2) | copy-start | bytes 49156
  2198.8 0.6 copy-start.3
Sparse Core Ops, SparseCore 0:
  221.9 262.9 all-reduce.12
  625.8 99.6 all-gather.3
  877.3 20.9 reduce-scatter.3
  977.4 234.2 all-reduce.8
  1293.4 95.4 all-gather.5
  1538.0 20.9 reduce-scatter.5
  1639.0 234.2 all-reduce.10
  1955.0 95.4 all-gather.7
  2199.6 20.9 reduce-scatter.7
